TPU v7x, 256 devices: a whole 4x4x8 slice. The times are simulated.
256 devices in a mesh: dp: 16 (over y_lo, z), fsdp: 16 (over x, y_hi, core).
Axes of the slice: x: 4, y: 4 (y_hi: 2, y_lo: 2; y = y_hi * 2 + y_lo), z: 8, core: 2. Of those that a mesh axis runs over, the one named last changes fastest.
Arguments:
- frames: bfloat16 [256, 256, 1536], P(('dp', 'fsdp')), may hold values from -6 to 6
- cotangent: bfloat16 [256, 256, 1536], P(('dp', 'fsdp')), may hold values from -6 to 6
- lengths: int32 [256], P(('dp', 'fsdp')), may hold values from 64 to 256, as said below
- weight_slots: bfloat16 [2304, 3072], P('fsdp'), may hold values from -0.15625 to 0.15625
- owner_rows: int32 [2304], replicated, may hold values from -1 to 1535, as said below
- gain_in: float32 [1536], replicated, may hold values from 0.5 to 1.5
- gain_mid: float32 [1536], replicated, may hold values from 0.5 to 1.5
- kernel: float32 [32, 1536], replicated, may hold values from -1 to 1
Outputs:
- frame_grads: bfloat16 [256, 256, 1536], P(('dp', 'fsdp'))
- weight_grads: bfloat16 [2304, 3072], P('fsdp')
- gain_in_grad: float32 [1536], replicated
- gain_mid_grad: float32 [1536], replicated
- kernel_grad: float32 [32, 1536], replicated
Inputs may be any that keep to these rules, and one draw needn't show every extreme that they name: `owner_rows`: slots o * 144 to o * 144 + 143 belong to owner o (index o of fsdp): first the rows it holds, then -1. Each of the 1536 rows is named by exactly one slot. An owner holds between 48 and 144 rows, and some owner holds exactly 144. Rows of weight_slots in slots marked -1 are not used. `lengths`: some utterance has all 256 frames in use.
All inputs are finite; a program needn't handle non-finite values.
Results may differ from a plain program's by a relative error of at most 0.02.
Values may be sent and summed in bfloat16 or wider, within the bound.
A program may use at most 192 MiB of HBM per device.

v0:
```python
import jax
import jax.numpy as jnp
from jax import lax
from jax.sharding import PartitionSpec as P

EPSILON = 1e-05


def norm_rows(values, scales):
    row_mean = jnp.mean(values, axis=-1, keepdims=True)
    centred = values - row_mean
    spread = jnp.mean(centred * centred, axis=-1, keepdims=True)
    return centred * lax.rsqrt(spread + EPSILON) * scales


def branch_tail(projected, gain_mid, kernel, frame_keep):
    features = gain_mid.shape[0]
    kernel_taps = kernel.shape[0]
    gated = (
        projected[..., :features]
        * jax.nn.sigmoid(projected[..., features:])
        * frame_keep[..., None]
    )
    length = gated.shape[1]
    left_pad = kernel_taps // 2
    padded = jnp.pad(gated, ((0, 0), (left_pad, kernel_taps - 1 - left_pad), (0, 0)))
    convolved = jnp.zeros_like(gated)
    for offset in range(kernel_taps):
        convolved = convolved + kernel[offset] * padded[:, offset : offset + length, :]
    mixed = norm_rows(convolved, gain_mid)
    return mixed * jax.nn.sigmoid(mixed) * frame_keep[..., None]


def per_device(frames, cotangent, lengths, weight_slots, owner_rows, gain_in, gain_mid, kernel):
    utterances, length, features = frames.shape
    token_rows = utterances * length
    slot_count = owner_rows.shape[0]
    valid_slot = owner_rows >= 0
    safe_rows = jnp.where(valid_slot, owner_rows, 0)
    valid_mask = valid_slot.astype(jnp.bfloat16)
    frame_keep = (jnp.arange(length)[None, :] < lengths[:, None]).astype(jnp.float32)
    frames_wide = frames.astype(jnp.float32)
    normed, head_back = jax.vjp(norm_rows, frames_wide, gain_in)
    normed_flat = normed.astype(jnp.bfloat16).reshape(token_rows, features)
    gathered = lax.all_gather(weight_slots, "fsdp", axis=0, tiled=True)
    inverse = (
        jnp.zeros((features,), jnp.int32)
        .at[jnp.where(valid_slot, owner_rows, features)]
        .set(jnp.arange(slot_count, dtype=jnp.int32), mode="drop")
    )
    weight = jnp.take(gathered, inverse, axis=0)
    projected = jnp.dot(normed_flat, weight, preferred_element_type=jnp.float32)
    projected = projected.reshape(utterances, length, 2 * features)
    cotangent_wide = cotangent.astype(jnp.float32)

    def run_tail(projected_in, mid_scales, taps_in):
        return branch_tail(projected_in, mid_scales, taps_in, frame_keep)

    branch, tail_back = jax.vjp(run_tail, projected, gain_mid, kernel)
    projected_grad, gain_mid_grad, kernel_grad = tail_back(cotangent_wide)
    grad_flat = projected_grad.astype(jnp.bfloat16).reshape(token_rows, 2 * features)
    normed_grad = lax.dot_general(
        grad_flat, weight, (((1,), (1,)), ((), ())), preferred_element_type=jnp.float32
    )
    frames_back, gain_in_grad = head_back(normed_grad.reshape(utterances, length, features))
    frame_grads = (cotangent_wide + frames_back).astype(jnp.bfloat16)
    owned_rows = lax.psum_scatter(
        lax.dot_general(
            jnp.take(normed_flat, safe_rows, axis=1) * valid_mask[None, :],
            grad_flat,
            (((0,), (0,)), ((), ())),
            preferred_element_type=jnp.float32,
        ).astype(jnp.bfloat16),
        "fsdp",
        scatter_dimension=0,
        tiled=True,
    )
    weight_sum = lax.psum(owned_rows, "dp").astype(jnp.float32)
    gain_in_total, gain_mid_total, kernel_total = lax.psum(
        (gain_in_grad, gain_mid_grad, kernel_grad), ("dp", "fsdp")
    )
    weight_grads = weight_sum.astype(jnp.bfloat16)
    return (frame_grads, weight_grads, gain_in_total, gain_mid_total, kernel_total)


def solution(mesh):
    in_specs = (
        P(("dp", "fsdp"), None, None),
        P(("dp", "fsdp"), None, None),
        P(("dp", "fsdp")),
        P("fsdp", None),
        P(),
        P(),
        P(),
        P(),
    )
    out_specs = (P(("dp", "fsdp"), None, None), P("fsdp", None), P(), P(), P())
    return jax.shard_map(
        per_device, mesh=mesh, in_specs=in_specs, out_specs=out_specs, check_vma=False
    )
```

profile of v0, /device:TPU:2, one launch (start us, length us, event | category | flops | bytes accessed | tf_op | source)
XLA Modules:
  0.0 746.2 jit_solution(6646918404065023754)
XLA Ops:
  8.6 1.3 convert_reduce_fusion
  11.7 7.4 gather_fusion.1
  19.1 9.0 %scatter_custom_fusion = s32[1536]{0:T(1024)S(1)} fusion(s32[2304]{0:T(1024)S(1)} %get-tuple-element.117, s32[2304]{0:T(1024)S(1)} %iota.9, s32[]{:T(128)} %constant.48.clone.1), kind=kCustom, calls=%fused_computation.195 | custom fusion | bytes 6148 | tf_op jit(solution)/shard_map/scatter | solution.py:49
  28.7 86.9 %all-gather.2.cloned.1.call-done = bf16[2304,3072]{1,0:T(8,128)(2,1)} async-done(((bf16[144,3072]{1,0:T(8,128)(2,1)}), bf16[2304,3072]{1,0:T(8,128)(2,1)}) %all-gather.2.cloned.1.call-update) | async-done | bytes 14155792 | tf_op jit(solution)/shard_map/all_gather | solution.py:45
  115.7 24.8 %gather_fusion = bf16[1536,3072]{1,0:T(8,128)(2,1)} fusion(bf16[2304,3072]{1,0:T(8,128)(2,1)} %all-gather.2.cloned.1.call-done, s32[2048]{0:T(1024)S(1)} %pad_clamp_fusion.1), kind=kCustom, calls=%fused_computation | custom fusion | bytes 18880512 | tf_op jit(solution)/shard_map/jit(_take)/gather | solution.py:51
  140.5 6.4 convolution_bitcast_fusion
  147.3 1.2 copy-done.2
  148.6 8.2 %fusion.44 = (f32[256]{0:T(256)S(1)}, f32[1,256,1536]{2,1,0:T(8,128)S(1)}) fusion(f32[1536]{0:T(1024)S(1)} %get-tuple-element.41, f32[1536]{0:T(1024)S(1)} %get-tuple-element.71, f32[1536]{0:T(1024)S(1)} %get-tuple-element.72, f32[1536]{0:T(1024)S(1)} %get-tuple-element.42, f32[1536]{0:T(1024)S(1)} %get-tuple-element.43, f32[1536]{0:T(1024)S(1)} %get-tuple-element.44, ...), kind=kLoop, calls=%fused_computation.216 | loop fusion | flops 25165568 | bytes 3343360 | tf_op jit(solution)/shard_map/jvp()/reduce_sum | solution.py:10
  157.9 1.8 multiply_reduce_fusion.32
  160.2 4.2 multiply_reduce_fusion.30
  164.4 9.1 %broadcast_multiply_fusion.31 = (f32[1,256,1536]{2,1,0:T(8,128)}, f32[1,256,1536]{2,1,0:T(8,128)}, f32[1,256,1536]{2,1,0:T(8,128)}, f32[1,256,1536]{2,1,0:T(8,12...) fusion(f32[1536]{0:T(1024)S(1)} %get-tuple-element.41, ...), kind=kLoop, calls=%fused_computation.149 | loop fusion | flops 7077888 | bytes 28417024 | tf_op jit(solution)/shard_map/transpose(jvp())/mul | solution.py:29
  173.5 7.2 broadcast_multiply_fusion
  180.7 14.8 %pad_add_fusion = f32[1,287,1536]{2,1,0:T(8,128)S(1)} fusion(f32[1,256,1536]{2,1,0:T(8,128)} %get-tuple-element.86, f32[1,256,1536]{2,1,0:T(8,128)} %get-tuple-element.87, f32[1,256,1536]{2,1,0:T(8,128)} %get-tuple-element.88, f32[1,256,1536]{2,1,0:T(8,128)} %get-tuple-element.89, f32[1,256,1536]{2,1,0:T(8,128)} %get-tuple-element.90, ...), kind=kLoop, calls=%fused_computation.24 | loop fusion | flops 11020800 | bytes 42657792 | tf_op jit(solution)/shard_map/transpose(jvp())/add_any | solution.py:29
  195.5 4.9 fusion.16
  202.6 7.9 %convolution_convert_fusion = bf16[2304,3072]{1,0:T(8,128)(2,1)} fusion(bf16[2304,256]{1,0:T(8,128)(2,1)S(1)} %copy-done.7, pred[2304]{0:T(1024)(128)(4,1)S(1)} %get-tuple-element.115, bf16[2304]{0:T(1024)(128)(2,1)S(1)} %get-tuple-element.114, f32[1,256,1536]{2,1,0:T(8,128)S(1)} %fusion.40, f32[1,256,1536]{2,1,0:T(8,128)S(1)} %get-tuple-element.75), kind=kOutput, calls=%fused_computation.3 | convolution fusion | flops 3633709056 | bytes 18488064 | tf_op jit(solution)/shard_map/dot_general | solution.py:68
  211.2 5.0 multiply_reduce_fusion.31
  216.5 1.0 pad_add_fusion.7
  217.5 8.3 %fusion.15 = (f32[256]{0:T(256)S(1)}, f32[256,1536]{1,0:T(8,128)S(1)}) fusion(bf16[1,256,1536]{2,1,0:T(8,128)(2,1)} %param.8, f32[1536]{0:T(1024)S(1)} %copy-done.12, f32[256]{0:T(256)S(1)} %copy-done.19, bf16[1536,3072]{1,0:T(8,128)(2,1)} %gather_fusion, pred[1536]{0:T(1024)(128)(4,1)S(1)} %copy-done.27, f32[1,256,1536]{2,1,0:T(8,128)} %copy-done.6, ...), kind=kOutput, calls=%fused_computation.62 | convolution fusion | flops 2424176384 | bytes 14951936 | tf_op jit(solution)/shard_map/dot_general | solution.py:62
  225.9 120.1 %reduce-scatter.2.cloned.1.call-done = bf16[144,3072]{1,0:T(8,128)(2,1)} async-done(((bf16[2304,3072]{1,0:T(8,128)(2,1)}), bf16[144,3072]{1,0:T(8,128)(2,1)}) %reduce-scatter.2.cloned.1.call-update) | async-done | bytes 884752 | tf_op jit(solution)/shard_map/reduce_scatter | solution.py:67
  346.9 74.4 %all-reduce.67 = (f32[1536]{0:T(1024)}, f32[1536]{0:T(1024)}) all-reduce(f32[1536]{0:T(1024)S(1)} %get-tuple-element.39, f32[1536]{0:T(1024)S(1)} %copy-done.15), channel_id=1, replica_groups=mesh['dp'=16,'fsdp'=16] {'dp','fsdp'}, use_global_device_ids=true, to_apply=%region_12.13 | all-reduce | flops 3072 | bytes 24576 | tf_op jit(solution)/shard_map/psum | solution.py:79
  421.3 1.5 fusion.13
  422.8 175.4 %all-reduce.73.cloned.1.call-done = f32[32,1536]{1,0:T(8,128)} async-done(((f32[32,1536]{1,0:T(8,128)}), f32[32,1536]{1,0:T(8,128)}) %all-reduce.73.cloned.1.call-update) | async-done | bytes 196624 | tf_op jit(solution)/shard_map/psum | solution.py:79
  598.2 138.6 %all-reduce.71.cloned.1.call-done = bf16[144,3072]{1,0:T(8,128)(2,1)} async-done(((bf16[144,3072]{1,0:T(8,128)(2,1)}), bf16[144,3072]{1,0:T(8,128)(2,1)}) %all-reduce.71.cloned.1.call-update) | async-done | bytes 884752 | tf_op jit(solution)/shard_map/psum | solution.py:78
  736.8 2.1 copy.17
  (122 shorter events, 9.4 us)
Async XLA Ops:
  7.2 2.8 copy-start
  7.2 3.7 copy-start.12
  7.2 108.5 %all-gather.2.cloned.1.call-start = ((), (), s32[]{:S(2)}) async-start(), calls=%async_computation.1 | async-start | bytes 15040512 | tf_op jit(solution)/shard_map/all_gather | solution.py:45
  7.9 338.1 %reduce-scatter.2.cloned.1.call-start = ((), (), s32[]{:S(2)}) async-start(), calls=%async_computation.2 | async-start | bytes 15040512 | tf_op jit(solution)/shard_map/reduce_scatter | solution.py:67
  10.0 1.6 copy-start.18
  11.7 16.5 %copy-start.11 = (f32[32,1536]{1,0:T(8,128)S(1)}, f32[32,1536]{1,0:T(8,128)}, u32[]{:S(2)}) copy-start(f32[32,1536]{1,0:T(8,128)} %param.15) | copy-start | bytes 589828
  28.1 129.0 %copy-start.22 = (f32[256]{0:T(256)}, f32[256]{0:T(256)S(1)}, u32[]{:S(2)}) copy-start(f32[256]{0:T(256)S(1)} %compare_convert_fusion.1) | copy-start | bytes 3076
  28.7 111.8 %copy-start.26 = (pred[1536]{0:T(1024)(128)(4,1)}, pred[1536]{0:T(1024)(128)(4,1)S(1)}, u32[]{:S(2)}) copy-start(pred[1536]{0:T(1024)(128)(4,1)S(1)} %compare_and_fusion.1) | copy-start | bytes 4612
  146.9 1.7 copy-start.2
  160.2 13.3 %copy-start.16 = (f32[256]{0:T(256)}, f32[256]{0:T(256)S(1)}, u32[]{:S(2)}) copy-start(f32[256]{0:T(256)S(1)} %negate_multiply_fusion.1) | copy-start | bytes 3076
  180.7 14.8 %copy-start.3 = (f32[1,256,3072]{2,1,0:T(8,128)S(1)}, f32[1,256,3072]{2,1,0:T(8,128)}, u32[]{:S(2)}) copy-start(f32[1,256,3072]{2,1,0:T(8,128)} %copy-done.2) | copy-start | bytes 9437188
  180.7 14.8 %copy-start.5 = (f32[1,256,1536]{2,1,0:T(8,128)S(1)}, f32[1,256,1536]{2,1,0:T(8,128)}, u32[]{:S(2)}) copy-start(f32[1,256,1536]{2,1,0:T(8,128)} %get-tuple-element.85) | copy-start | bytes 4718596
  180.7 14.8 %copy-start.23 = (f32[256]{0:T(256)S(1)}, f32[256]{0:T(256)}, u32[]{:S(2)}) copy-start(f32[256]{0:T(256)} %copy-done.22) | copy-start | bytes 3076
  200.4 1.2 copy-start.4
  200.5 2.1 copy-start.7
  210.6 387.6 %all-reduce.73.cloned.1.call-start = ((), (), s32[]{:S(2)}) async-start(), calls=%async_computation.4 | async-start | bytes 393216 | tf_op jit(solution)/shard_map/psum | solution.py:79
  211.2 6.3 copy-start.19
  211.2 6.3 copy-start.27
  217.5 8.4 %copy-start.25 = (f32[256]{0:T(256)S(1)}, f32[256]{0:T(256)}, u32[]{:S(2)}) copy-start(f32[256]{0:T(256)} %copy-done.24) | copy-start | bytes 3076
  217.5 128.5 %copy-start.21 = (f32[256]{0:T(256)S(1)}, f32[256]{0:T(256)}, u32[]{:S(2)}) copy-start(f32[256]{0:T(256)} %copy-done.20) | copy-start | bytes 3076
  225.8 120.2 %copy-start.1 = (bf16[1,256,1536]{2,1,0:T(8,128)(2,1)S(1)}, bf16[1,256,1536]{2,1,0:T(8,128)(2,1)}, u32[]{:S(2)}) copy-start(bf16[1,256,1536]{2,1,0:T(8,128)(2,1)} %param.8) | copy-start | bytes 2359300
  225.9 510.9 %all-reduce.71.cloned.1.call-start = ((), (), s32[]{:S(2)}) async-start(), calls=%async_computation.3 | async-start | bytes 1769472 | tf_op jit(solution)/shard_map/psum | solution.py:78
  346.0 75.3 %copy-start.9 = (bf16[1,256,1536]{2,1,0:T(8,128)(2,1)S(1)}, bf16[1,256,1536]{2,1,0:T(8,128)(2,1)}, u32[]{:S(2)}) copy-start(bf16[1,256,1536]{2,1,0:T(8,128)(2,1)} %param.9) | copy-start | bytes 2359300
  598.2 140.8 %copy-start.10 = (f32[32,1536]{1,0:T(8,128)S(1)}, f32[32,1536]{1,0:T(8,128)}, u32[]{:S(2)}) copy-start(f32[32,1536]{1,0:T(8,128)} %all-reduce.73.cloned.1.call-done) | copy-start | bytes 589828
  (8 other events, 6.9 us)
Sparse Core Ops, SparseCore 0:
  10.7 104.8 all-gather.1
  210.7 135.3 reduce-scatter.1
  353.0 245.1 all-reduce.72
  600.9 135.8 all-reduce.70
where the time goes:
time: 747 us; the launch traced here: 746 us
  waiting for transfers between devices  522 us (70%)
  blocking collectives  74.4 us (10%)
  other arithmetic  62.2 us (8%)
  local copies, waits for them, and re-layouts  49.9 us (7%)
  matrix products  22.6 us (3%)
  between operations  15.1 us (2%)
    psum x1, waiting for transfers between devices, per_device(): lax.psum((gain_in_grad, gain_mid_grad, kernel_grad), ('dp', 'fsdp'))  175 us
    psum x1, waiting for transfers between devices, per_device(): weight_sum = lax.psum(owned_rows, 'dp').astype(jnp.float32)  139 us
    reduce_scatter x1, waiting for transfers between devices, per_device(): lax.psum_scatter(lax.dot_general(jnp.take(normed_flat, safe_rows, axis=1)...  120 us
    all_gather x1, waiting for transfers between devices, per_device(): gathered = lax.all_gather(weight_slots, 'fsdp', axis=0, tiled=True)  86.9 us
    psum x1, blocking collectives, per_device(): lax.psum((gain_in_grad, gain_mid_grad, kernel_grad), ('dp', 'fsdp'))  74.4 us
    gather x1, local copies, waits for them, and re-layouts, per_device(): weight = jnp.take(gathered, inverse, axis=0)  24.8 us
    mul x2, other arithmetic, branch_tail(): kernel[offset] * padded[:, offset:offset + length, :]  16.3 us
  transfers between devices with their start and end apart: 4, of which 4 were waited for; matrix products, arithmetic and copies ran while one was open for 5% of the time, Pallas kernels for 0%

commit v1 on v0

--- a/solution.py
+++ b/solution.py
@@ -75,7 +75,7 @@
         scatter_dimension=0,
         tiled=True,
     )
-    weight_sum = lax.psum(owned_rows, "dp").astype(jnp.float32)
+    weight_sum = jnp.sum(lax.all_gather(owned_rows, "dp"), axis=0).astype(jnp.float32)
     gain_in_total, gain_mid_total, kernel_total = lax.psum(
         (gain_in_grad, gain_mid_grad, kernel_grad), ("dp", "fsdp")
     )

time: 747 us -> 772 us (1.033)
  blocking collectives: 74.4 us -> 209 us
  waiting for transfers between devices: 522 us -> 399 us
  other arithmetic: 62.2 us -> 72.7 us
    psum x1 -> x0, waiting for transfers between devices: 139 us -> none  [per_device(): weight_sum = lax.psum(owned_rows, 'dp').astype(jnp.float32)]
    psum x1, blocking collectives: 74.4 us -> 209 us  [per_device(): lax.psum((gain_in_grad, gain_mid_grad, kernel_grad), ('dp', 'fsdp'))]
    reduce_scatter x1, waiting for transfers between devices: 120 us -> 135 us  [per_device(): lax.psum_scatter(lax.dot_general(jnp.take(normed_flat, safe_rows, axis=1)...]
    reduce_sum x0 -> x1, other arithmetic: none -> 9.28 us  [per_device(): jnp.sum(lax.all_gather(owned_rows, 'dp'), axis=0).astype(jnp.float32)]
  transfers between devices with their start and end apart: 4 -> 4, of which waited for: 4 -> 3; matrix products, arithmetic and copies ran while one was open for 5% -> 6% of each run, Pallas kernels for 0% -> 0%
where the time goes in v1:
time: 772 us; the launch traced here: 767 us
  waiting for transfers between devices  399 us (52%)
  blocking collectives  209 us (27%)
  other arithmetic  72.7 us (9%)
  local copies, waits for them, and re-layouts  49.4 us (6%)
  matrix products  20.9 us (3%)
  between operations  15.4 us (2%)
    psum x1, blocking collectives, per_device(): lax.psum((gain_in_grad, gain_mid_grad, kernel_grad), ('dp', 'fsdp'))  209 us
    psum x1, waiting for transfers between devices, per_device(): lax.psum((gain_in_grad, gain_mid_grad, kernel_grad), ('dp', 'fsdp'))  177 us
    reduce_scatter x1, waiting for transfers between devices, per_device(): lax.psum_scatter(lax.dot_general(jnp.take(normed_flat, safe_rows, axis=1)...  135 us
    all_gather x1, waiting for transfers between devices, per_device(): gathered = lax.all_gather(weight_slots, 'fsdp', axis=0, tiled=True)  86.2 us
    gather x1, local copies, waits for them, and re-layouts, per_device(): weight = jnp.take(gathered, inverse, axis=0)  25.1 us
    mul x2, other arithmetic, branch_tail(): kernel[offset] * padded[:, offset:offset + length, :]  17 us
  transfers between devices with their start and end apart: 4, of which 3 were waited for; matrix products, arithmetic and copies ran while one was open for 6% of the time, Pallas kernels for 0%

profile of v1, /device:TPU:2, one launch (start us, length us, event | category | flops | bytes accessed | tf_op | source)
XLA Modules:
  0.0 766.7 jit_solution(7691299890900381354)
XLA Ops:
  8.6 1.3 convert_reduce_fusion
  11.8 7.4 gather_fusion.1
  19.3 9.0 %scatter_custom_fusion = s32[1536]{0:T(1024)S(1)} fusion(s32[2304]{0:T(1024)S(1)} %get-tuple-element.117, s32[2304]{0:T(1024)S(1)} %iota.9, s32[]{:T(128)} %constant.49.clone.1), kind=kCustom, calls=%fused_computation.195 | custom fusion | bytes 6148 | tf_op jit(solution)/shard_map/scatter | solution.py:49
  29.5 86.2 %all-gather.4.cloned.1.call-done = bf16[2304,3072]{1,0:T(8,128)(2,1)} async-done(((bf16[144,3072]{1,0:T(8,128)(2,1)}), bf16[2304,3072]{1,0:T(8,128)(2,1)}) %all-gather.4.cloned.1.call-update) | async-done | bytes 14155792 | tf_op jit(solution)/shard_map/all_gather | solution.py:45
  115.7 25.1 %gather_fusion = bf16[1536,3072]{1,0:T(8,128)(2,1)} fusion(bf16[2304,3072]{1,0:T(8,128)(2,1)} %all-gather.4.cloned.1.call-done, s32[2048]{0:T(1024)S(1)} %pad_clamp_fusion.1), kind=kCustom, calls=%fused_computation | custom fusion | bytes 18880512 | tf_op jit(solution)/shard_map/jit(_take)/gather | solution.py:51
  140.8 6.4 convolution_bitcast_fusion
  147.6 1.2 copy-done.3
  148.8 8.1 %fusion.44 = (f32[256]{0:T(256)S(1)}, f32[1,256,1536]{2,1,0:T(8,128)S(1)}) fusion(f32[1536]{0:T(1024)S(1)} %get-tuple-element.41, f32[1536]{0:T(1024)S(1)} %get-tuple-element.71, f32[1536]{0:T(1024)S(1)} %get-tuple-element.72, f32[1536]{0:T(1024)S(1)} %get-tuple-element.42, f32[1536]{0:T(1024)S(1)} %get-tuple-element.43, f32[1536]{0:T(1024)S(1)} %get-tuple-element.44, ...), kind=kLoop, calls=%fused_computation.216 | loop fusion | flops 25165568 | bytes 3343360 | tf_op jit(solution)/shard_map/jvp()/reduce_sum | solution.py:10
  158.1 1.2 multiply_reduce_fusion.32
  160.4 4.3 multiply_reduce_fusion.30
  164.8 9.8 %broadcast_multiply_fusion.31 = (f32[1,256,1536]{2,1,0:T(8,128)}, f32[1,256,1536]{2,1,0:T(8,128)}, f32[1,256,1536]{2,1,0:T(8,128)}, f32[1,256,1536]{2,1,0:T(8,12...) fusion(f32[1536]{0:T(1024)S(1)} %get-tuple-element.41, ...), kind=kLoop, calls=%fused_computation.149 | loop fusion | flops 7077888 | bytes 28417024 | tf_op jit(solution)/shard_map/transpose(jvp())/mul | solution.py:29
  174.6 7.2 broadcast_multiply_fusion
  181.8 14.8 %pad_add_fusion = f32[1,287,1536]{2,1,0:T(8,128)S(1)} fusion(f32[1,256,1536]{2,1,0:T(8,128)} %get-tuple-element.86, f32[1,256,1536]{2,1,0:T(8,128)} %get-tuple-element.87, f32[1,256,1536]{2,1,0:T(8,128)} %get-tuple-element.88, f32[1,256,1536]{2,1,0:T(8,128)} %get-tuple-element.89, f32[1,256,1536]{2,1,0:T(8,128)} %get-tuple-element.90, ...), kind=kLoop, calls=%fused_computation.24 | loop fusion | flops 11020800 | bytes 42657792 | tf_op jit(solution)/shard_map/transpose(jvp())/add_any | solution.py:29
  196.6 5.4 fusion.16
  204.1 7.9 %convolution_convert_fusion = bf16[2304,3072]{1,0:T(8,128)(2,1)} fusion(bf16[2304,256]{1,0:T(8,128)(2,1)S(1)} %copy-done.8, pred[2304]{0:T(1024)(128)(4,1)S(1)} %copy-done.15, bf16[2304]{0:T(1024)(128)(2,1)S(1)} %get-tuple-element.114, f32[1,256,1536]{2,1,0:T(8,128)S(1)} %fusion.40, f32[1,256,1536]{2,1,0:T(8,128)S(1)} %get-tuple-element.75), kind=kOutput, calls=%fused_computation.3 | convolution fusion | flops 3633709056 | bytes 18488064 | tf_op jit(solution)/shard_map/dot_general | solution.py:68
  212.1 135.4 %reduce-scatter.2.cloned.1.call-done = bf16[144,3072]{1,0:T(8,128)(2,1)} async-done(((bf16[2304,3072]{1,0:T(8,128)(2,1)}), bf16[144,3072]{1,0:T(8,128)(2,1)}) %reduce-scatter.2.cloned.1.call-update) | async-done | bytes 884752 | tf_op jit(solution)/shard_map/reduce_scatter | solution.py:67
  347.9 5.0 multiply_reduce_fusion.31
  353.2 6.6 fusion.15
  360.7 1.0 pad_add_fusion.7
  361.8 1.5 fusion.13
  363.3 209.2 %all-reduce.67 = (f32[1536]{0:T(1024)}, f32[1536]{0:T(1024)}) all-reduce(f32[1536]{0:T(1024)S(1)} %get-tuple-element.39, f32[1536]{0:T(1024)S(1)} %get-tuple-element.37), channel_id=1, replica_groups=mesh['dp'=16,'fsdp'=16] {'dp','fsdp'}, use_global_device_ids=true, to_apply=%region_12.13 | all-reduce | flops 3072 | bytes 24576 | tf_op jit(solution)/shard_map/psum | solution.py:79
  572.5 9.3 %reduce_sum.394 = bf16[144,3072]{1,0:T(8,128)(2,1)} reduce(bf16[16,144,3072]{2,1,0:T(8,128)(2,1)} %bitcast.24, bf16[]{:T(256)} %constant.57.clone.1), dimensions={0}, to_apply=%region_10.11 | reduce | flops 6635520 | bytes 15040514 | tf_op jit(solution)/shard_map/reduce_sum | solution.py:78
  581.8 176.6 %all-reduce.70.cloned.1.call-done = f32[32,1536]{1,0:T(8,128)} async-done(((f32[32,1536]{1,0:T(8,128)}), f32[32,1536]{1,0:T(8,128)}) %all-reduce.70.cloned.1.call-update) | async-done | bytes 196624 | tf_op jit(solution)/shard_map/psum | solution.py:79
  758.3 1.6 copy.16
  (122 shorter events, 9.7 us)
Async XLA Ops:
  7.2 2.8 copy-start
  7.2 3.7 copy-start.12
  7.2 108.5 %all-gather.4.cloned.1.call-start = ((), (), s32[]{:S(2)}) async-start(), calls=%async_computation.1 | async-start | bytes 15040512 | tf_op jit(solution)/shard_map/all_gather | solution.py:45
  7.9 339.7 %reduce-scatter.2.cloned.1.call-start = ((), (), s32[]{:S(2)}) async-start(), calls=%async_computation.2 | async-start | bytes 15040512 | tf_op jit(solution)/shard_map/reduce_scatter | solution.py:67
  10.0 1.3 copy-start.18
  11.8 16.5 %copy-start.11 = (f32[32,1536]{1,0:T(8,128)S(1)}, f32[32,1536]{1,0:T(8,128)}, u32[]{:S(2)}) copy-start(f32[32,1536]{1,0:T(8,128)} %param.15) | copy-start | bytes 589828
  28.3 129.0 %copy-start.22 = (f32[256]{0:T(256)}, f32[256]{0:T(256)S(1)}, u32[]{:S(2)}) copy-start(f32[256]{0:T(256)S(1)} %compare_convert_fusion.1) | copy-start | bytes 3076
  28.9 111.9 %copy-start.26 = (pred[1536]{0:T(1024)(128)(4,1)}, pred[1536]{0:T(1024)(128)(4,1)S(1)}, u32[]{:S(2)}) copy-start(pred[1536]{0:T(1024)(128)(4,1)S(1)} %compare_and_fusion.1) | copy-start | bytes 4612
  147.2 1.7 copy-start.3
  164.8 9.8 %copy-start.17 = (f32[256]{0:T(256)S(1)}, f32[256]{0:T(256)}, u32[]{:S(2)}) copy-start(f32[256]{0:T(256)} %copy-done.16) | copy-start | bytes 3076
  181.8 14.8 %copy-start.4 = (f32[1,256,3072]{2,1,0:T(8,128)S(1)}, f32[1,256,3072]{2,1,0:T(8,128)}, u32[]{:S(2)}) copy-start(f32[1,256,3072]{2,1,0:T(8,128)} %copy-done.3) | copy-start | bytes 9437188
  181.8 14.8 %copy-start.23 = (f32[256]{0:T(256)S(1)}, f32[256]{0:T(256)}, u32[]{:S(2)}) copy-start(f32[256]{0:T(256)} %copy-done.22) | copy-start | bytes 3076
  202.0 2.1 copy-start.8
  202.0 2.1 copy-start.15
  212.1 360.4 %all-gather.6.cloned.1.call-start = ((), (), s32[]{:S(2)}) async-start(), calls=%async_computation.4 | async-start | bytes 15040512 | tf_op jit(solution)/shard_map/all_gather | solution.py:78
  347.6 410.7 %all-reduce.70.cloned.1.call-start = ((), (), s32[]{:S(2)}) async-start(), calls=%async_computation.3 | async-start | bytes 393216 | tf_op jit(solution)/shard_map/psum | solution.py:79
  347.9 5.3 copy-start.1
  347.9 5.3 copy-start.6
  347.9 5.3 copy-start.19
  347.9 5.3 copy-start.27
  353.2 6.7 copy-start.25
  353.2 6.7 copy-start.21
  359.8 1.9 copy-start.2
  359.9 1.9 copy-start.10
  (8 other events, 7.3 us)
Sparse Core Ops, SparseCore 0:
  10.7 104.8 all-gather.3
  212.2 135.3 reduce-scatter.1
  349.5 158.1 all-gather.5
  514.6 243.7 all-reduce.69
